TPU v7x, 128 devices: a whole 4x4x4 slice. The times are simulated.
128 devices in a mesh: det: 8 (over y, core), patch: 16 (over z, x).
Axes of the slice: x: 4, y: 4, z: 4, core: 2. Of those that a mesh axis runs over, the one named last changes fastest.
Arguments:
- exposure: bfloat16 [32768, 4096], P(('det', 'patch')), may hold values from -8 to 8
- block_dest: int32 [4096], P(('det', 'patch')), may hold values from 0 to 4095, as said below
- band_offset: int32 [4096], P(('det', 'patch')), may hold values from -8 to 8
- col_shift: float32 [4096], P(('det', 'patch')), may hold values from 0.05 to 0.95
- block_weight: float32 [4096], P(('det', 'patch')), may hold values from 0.5 to 4
- basis_width: float32 [3], replicated, may hold values from 1 to 5
- kernel_fit: float32 [128, 3, 6], P(('det', 'patch')), may hold values from -3 to 3
- fit_owner: int32 [1], replicated, may hold values from 0 to 127
Outputs:
- matched: bfloat16 [32768, 4096], P(('det', 'patch'))
- coverage: float32 [4096], P(('det', 'patch'))
Inputs may be any that keep to these rules, and one draw needn't show every extreme that they name: `block_dest`: block b of device d (b in d * 32 .. d * 32 + 31) lands in a slot of a device of d's det group (slots d' 32 .. d' 32 + 31 belong to device d'); no device sends more than 3 of its blocks to one device, and every device sends exactly 3 to some device.
All inputs are finite; a program needn't handle non-finite values.
Results may differ from a plain program's by a relative error of at most 0.013.
Values may be sent and summed in bfloat16 or wider, within the bound.
A program may use at most 448 MiB of HBM per device.

v0:
```python
import jax
import jax.numpy as jnp
from jax import lax
from jax.sharding import PartitionSpec as P

TAPS = 31
BASES = 3
TILE = 512


def spread(value, axis, root):
    mine = lax.axis_index(axis) == root
    return lax.psum(jnp.where(mine, value, jnp.zeros_like(value)), axis)


def with_halo(block, sides, width):
    for axis, dim in sides:
        count = lax.axis_size(axis)
        forward = [(i, i + 1) for i in range(count - 1)]
        backward = [(target, source) for source, target in forward]
        low = lax.ppermute(
            lax.slice_in_dim(block, block.shape[dim] - width, None, axis=dim), axis, forward
        )
        high = lax.ppermute(lax.slice_in_dim(block, 0, width, axis=dim), axis, backward)
        block = jnp.concatenate([low, block, high], axis=dim)
    return block


def lanczos(position):
    return jnp.sinc(position) * jnp.sinc(position / 3.0)


def resample_blocks(source_rows, offsets, shifts, weights):
    col_count = source_rows.shape[2]
    column_margin = 128
    padded = jnp.pad(source_rows, ((0, 0), (0, 0), (column_margin, column_margin)))
    summed = jnp.zeros(source_rows.shape, jnp.float32)
    for shift_value in range(-10, 12):
        coeffs = jnp.zeros(shifts.shape, jnp.float32)
        for offset_tap in range(-2, 4):
            coeffs = coeffs + jnp.where(
                offsets + offset_tap == shift_value, lanczos(offset_tap - shifts), 0.0
            )
        start_col = column_margin + shift_value
        picked = padded[:, :, start_col : start_col + col_count]
        summed = summed + coeffs[:, None, None] * picked.astype(jnp.float32)
    return summed * weights[:, None, None]


def gaussian_taps(basis_width):
    half_span = (TAPS - 1) // 2
    positions = jnp.arange(TAPS).astype(jnp.float32) - half_span
    profile = jnp.exp(-positions[None, :] ** 2 / (2.0 * basis_width[:, None] ** 2))
    return profile / jnp.sum(profile, axis=1, keepdims=True)


def poly_field(coeff_row, row_pos, col_pos):
    yy_pos = row_pos[:, None]
    xx_pos = col_pos[None, :]
    return (
        coeff_row[0]
        + coeff_row[1] * xx_pos
        + coeff_row[2] * yy_pos
        + coeff_row[3] * xx_pos * xx_pos
        + coeff_row[4] * xx_pos * yy_pos
        + coeff_row[5] * yy_pos * yy_pos
    )


def band_table(taps_row, tile_step):
    half_span = (TAPS - 1) // 2
    differ = jnp.arange(TILE)[:, None] - jnp.arange(TILE)[None, :] + tile_step * TILE + half_span
    table = jnp.zeros((TILE, TILE), jnp.float32)
    for tap_index in range(TAPS):
        table = table + jnp.where(differ == tap_index, taps_row[tap_index].astype(jnp.float32), 0.0)
    return table.astype(jnp.bfloat16)


def column_convolve(image_rows, taps_row):
    row_count, col_count = image_rows.shape
    tile_count = col_count // TILE
    tiles = image_rows.reshape(row_count, tile_count, TILE)
    zero_tile = jnp.zeros((row_count, 1, TILE), image_rows.dtype)
    before = jnp.concatenate([zero_tile, tiles[:, :-1]], axis=1)
    after = jnp.concatenate([tiles[:, 1:], zero_tile], axis=1)
    smoothed = jnp.einsum(
        "rna,ab->rnb", tiles, band_table(taps_row, 0), preferred_element_type=jnp.float32
    )
    smoothed = smoothed + jnp.einsum(
        "rna,ab->rnb", before, band_table(taps_row, -1), preferred_element_type=jnp.float32
    )
    smoothed = smoothed + jnp.einsum(
        "rna,ab->rnb", after, band_table(taps_row, 1), preferred_element_type=jnp.float32
    )
    return smoothed.reshape(row_count, col_count)


def row_convolve(rimmed, taps_row, row_count):
    result = jnp.zeros((row_count, rimmed.shape[1]), jnp.float32)
    for tap_index in range(TAPS):
        result = result + taps_row[tap_index] * rimmed[tap_index : tap_index + row_count]
    return result


def shards(
    exposure, block_dest, band_offset, col_shift, block_weight, basis_width, kernel_fit, fit_owner
):
    rows_dev, col_count = exposure.shape
    num_blocks = block_dest.shape[0]
    block_rows = rows_dev // num_blocks
    peers = lax.axis_size("patch")
    capacity = num_blocks // peers + 1
    source_blocks = exposure.reshape(num_blocks, block_rows, col_count)
    dest_local = block_dest % num_blocks
    dest_peer = block_dest // num_blocks % peers
    peer_onehot = (dest_peer[:, None] == jnp.arange(peers)[None, :]).astype(jnp.int32)
    rank_in_peer = jnp.sum((jnp.cumsum(peer_onehot, axis=0) - peer_onehot) * peer_onehot, axis=1)
    position = dest_peer * capacity + rank_in_peer
    select = jnp.arange(peers * capacity)[:, None] == position[None, :]
    select_bf = select.astype(jnp.bfloat16)
    slot_sent = jnp.sum(jnp.where(select, dest_local[None, :] + 1, 0), axis=1) - 1
    weight_sent = jnp.sum(jnp.where(select, block_weight[None, :], 0.0), axis=1)
    weighted = resample_blocks(source_blocks, band_offset, col_shift, block_weight).astype(
        jnp.bfloat16
    )
    packed = jnp.einsum(
        "ib,brw->irw", select_bf, weighted, preferred_element_type=jnp.float32
    ).astype(jnp.bfloat16)
    arrived, slot_got, weight_got = (
        lax.all_to_all(packed, "patch", split_axis=0, concat_axis=0, tiled=True),
        lax.all_to_all(slot_sent, "patch", split_axis=0, concat_axis=0, tiled=True),
        lax.all_to_all(
            weight_sent.astype(jnp.bfloat16), "patch", split_axis=0, concat_axis=0, tiled=True
        ).astype(weight_sent.dtype),
    )
    slot_match = jnp.arange(num_blocks)[:, None] == slot_got[None, :]
    coadd_sum = jnp.einsum(
        "si,irw->srw", slot_match.astype(jnp.bfloat16), arrived, preferred_element_type=jnp.float32
    )
    coverage = jnp.sum(jnp.where(slot_match, weight_got[None, :], 0.0), axis=1)
    image = (
        (coadd_sum / jnp.maximum(coverage, 1.0)[:, None, None])
        .astype(jnp.bfloat16)
        .reshape(rows_dev, col_count)
    )
    half_span = (TAPS - 1) // 2
    profile = gaussian_taps(basis_width)
    col_taps = profile.astype(jnp.bfloat16)
    chosen = spread(kernel_fit, ("det", "patch"), fit_owner[0])
    coeff = chosen[0]
    global_start = lax.axis_index(("det", "patch")) * rows_dev
    all_rows = rows_dev * lax.axis_size(("det", "patch"))
    row_pos = 2.0 * (global_start + jnp.arange(rows_dev)).astype(jnp.float32) / (all_rows - 1) - 1.0
    col_pos = 2.0 * jnp.arange(col_count).astype(jnp.float32) / (col_count - 1) - 1.0
    rimmed = with_halo(image, ((("det", "patch"), 0),), half_span)
    smoothed_list = [column_convolve(rimmed, col_taps[basis_index]) for basis_index in range(BASES)]
    matched = jnp.zeros((rows_dev, col_count), jnp.float32)
    for basis_index in range(BASES):
        rowconv = row_convolve(smoothed_list[basis_index], profile[basis_index], rows_dev)
        matched = matched + poly_field(coeff[basis_index], row_pos, col_pos) * rowconv
    return (matched.astype(jnp.bfloat16), coverage)


def solution(mesh):
    in_specs = (
        P(("det", "patch"), None),
        P(("det", "patch")),
        P(("det", "patch")),
        P(("det", "patch")),
        P(("det", "patch")),
        P(),
        P(("det", "patch"), None, None),
        P(),
    )
    out_specs = (P(("det", "patch"), None), P(("det", "patch")))
    return jax.shard_map(shards, mesh=mesh, in_specs=in_specs, out_specs=out_specs, check_vma=False)
```

profile of v0, /device:TPU:1, one launch (start us, length us, event | category | flops | bytes accessed | tf_op | source)
XLA Modules:
  0.0 863.3 jit_solution(13222734512006498839)
XLA Ops:
  3.1 8.4 all-to-all-start.2
  16.6 29.8 %convolution_convert_fusion = bf16[48,8,4096]{2,0,1:T(8,128)(2,1)S(1)} fusion(bf16[32,8,4096]{2,0,1:T(8,128)(2,1)} %copy.21, f32[32]{0:T(128)S(1)} %copy-done.61, f32[32]{0:T(128)S(1)} %get-tuple-element.81, f32[32]{0:T(128)S(1)} %get-tuple-element.62, f32[32]{0:T(128)S(1)} %get-tuple-element.63, f32[32]{0:T(128)S(1)} %get-tuple-element.64, ...), kind=kOutput, calls=%fused_computation | convolution fusion | flops 172492288 | bytes 5245952 | tf_op jit(solution)/shard_map/ib,brw->irw/dot_general | solution.py:126
  63.9 98.6 %psum.7 = f32[1,3,6]{2,0,1:T(1,128)S(1)} all-reduce(f32[1,3,6]{2,0,1:T(1,128)S(1)} %broadcast_select_fusion), channel_id=1, replica_groups=mesh['det'=8,'patch'=16] {'det','patch'}, use_global_device_ids=true, to_apply=%region_0.1 | all-reduce | flops 18 | bytes 144 | tf_op jit(solution)/shard_map/psum | solution.py:13
  271.4 7.8 fusion.54
  285.6 8.2 fusion.50
  301.6 19.3 %slice_multiply_fusion.45 = (f32[256,8,512]{2,1,0:T(8,128)}, f32[256,8,512]{2,1,0:T(8,128)}, f32[256,8,512]{2,1,0:T(8,128)}, f32[256,8,512]{2,1,0:T(8,128)}, f32...) fusion(f32[286,8,512]{2,1,0:T(8,128)S(1)} %add_add_fusion.1, ...), kind=kLoop, calls=%fused_computation.66 | loop fusion | flops 9437184 | bytes 75497504 | tf_op jit(solution)/shard_map/mul | solution.py:101
  320.9 8.2 copy.48
  383.3 34.3 %slice_multiply_fusion.76 = (f32[256,8,512]{2,1,0:T(8,128)}, f32[256,8,512]{2,1,0:T(8,128)}, f32[256,8,512]{2,1,0:T(8,128)}, f32[256,8,512]{2,1,0:T(8,128)}, f32...) fusion(f32[286,8,512]{2,1,0:T(8,128)} %add_add_fusion.2, ...), kind=kLoop, calls=%fused_computation.112 | loop fusion | flops 9437184 | bytes 75497504 | tf_op jit(solution)/shard_map/mul | solution.py:101
  417.6 8.1 copy.32
  473.6 12.5 %slice_multiply_fusion.44 = (f32[256,8,512]{2,1,0:T(8,128)}, f32[256,8,512]{2,1,0:T(8,128)}, f32[256,8,512]{2,1,0:T(8,128)}, f32[256,8,512]{2,1,0:T(8,128)}, f32[256,8,512]{2,1,0:T(8,128)}, /*index=5*/f32[256,8,512]{2,1,0:T(8,128)}) fusion(f32[286,8,512]{2,1,0:T(8,128)S(1)} %add_add_fusion.1, f32[]{:T(128)} %bitcast.134, f32[]{:T(128)} %bitcast.139, ...), kind=kLoop, calls=%fused_computation.65 | loop fusion | flops 6291456 | bytes 50331672 | tf_op jit(solution)/shard_map/mul | solution.py:101
  486.0 8.1 copy.49
  523.9 21.0 %slice_multiply_fusion.75 = (f32[256,8,512]{2,1,0:T(8,128)}, f32[256,8,512]{2,1,0:T(8,128)}, f32[256,8,512]{2,1,0:T(8,128)}, f32[256,8,512]{2,1,0:T(8,128)}, f32[256,8,512]{2,1,0:T(8,128)}, /*index=5*/f32[256,8,512]{2,1,0:T(8,128)}) fusion(f32[286,8,512]{2,1,0:T(8,128)} %add_add_fusion.2, f32[]{:T(128)} %bitcast.63, f32[]{:T(128)} %bitcast.68, f32[]{:T(128)} %bitcast.67, ...), kind=kLoop, calls=%fused_computation.111 | loop fusion | flops 6291456 | bytes 50331672 | tf_op jit(solution)/shard_map/mul | solution.py:101
  544.9 8.1 copy.33
  582.5 19.6 %fusion.16 = f32[256,8,512]{2,1,0:T(8,128)} fusion(f32[286,8,512]{2,1,0:T(8,128)S(1)} %add_add_fusion.1, f32[]{:T(128)} %bitcast.132, f32[]{:T(128)} %bitcast.131, f32[]{:T(128)} %bitcast.130, f32[]{:T(128)} %bitcast.129, f32[]{:T(128)} %bitcast.128, f32[]{:T(128)} %bitcast.127, f32[]{:T(128)} %bitcast.126, f32[]{:T(128)} %bitcast.125, f32[]{:T(128)} %bitcast.124, ...), kind=kLoop, calls=%fused_computation.68 | loop fusion | flops 32505856 | bytes 71303232 | tf_op jit(solution)/shard_map/add | solution.py:101
  602.1 8.2 copy.47
  610.3 19.8 %fusion.31 = f32[256,8,512]{2,1,0:T(8,128)} fusion(f32[286,8,512]{2,1,0:T(8,128)S(1)} %bitcast.446, f32[]{:T(128)} %bitcast.61, f32[]{:T(128)} %bitcast.60, f32[]{:T(128)} %bitcast.59, f32[]{:T(128)} %bitcast.58, f32[]{:T(128)} %bitcast.57, f32[]{:T(128)} %bitcast.56, f32[]{:T(128)} %bitcast.55, f32[]{:T(128)} %bitcast.54, f32[]{:T(128)} %bitcast.53, ...), kind=kLoop, calls=%fused_computation.114 | loop fusion | flops 32505856 | bytes 71303232 | tf_op jit(solution)/shard_map/add | solution.py:101
  630.2 8.2 copy.31
  645.9 19.5 %slice_multiply_fusion.14 = (f32[256,8,512]{2,1,0:T(8,128)}, f32[256,8,512]{2,1,0:T(8,128)}, f32[256,8,512]{2,1,0:T(8,128)}, f32[256,8,512]{2,1,0:T(8,128)}, f32...) fusion(f32[286,8,512]{2,1,0:T(8,128)S(1)} %add_add_fusion, ...), kind=kLoop, calls=%fused_computation.20 | loop fusion | flops 9437184 | bytes 75497504 | tf_op jit(solution)/shard_map/mul | solution.py:101
  665.4 8.2 copy.64
  721.2 12.3 %slice_multiply_fusion.13 = (f32[256,8,512]{2,1,0:T(8,128)}, f32[256,8,512]{2,1,0:T(8,128)}, f32[256,8,512]{2,1,0:T(8,128)}, f32[256,8,512]{2,1,0:T(8,128)}, f32[256,8,512]{2,1,0:T(8,128)}, /*index=5*/f32[256,8,512]{2,1,0:T(8,128)}) fusion(f32[286,8,512]{2,1,0:T(8,128)S(1)} %add_add_fusion, f32[]{:T(128)} %bitcast.205, f32[]{:T(128)} %bitcast.210, ...), kind=kLoop, calls=%fused_computation.19 | loop fusion | flops 6291456 | bytes 50331672 | tf_op jit(solution)/shard_map/mul | solution.py:101
  733.5 8.1 copy.65
  771.2 19.5 %fusion.1 = f32[256,8,512]{2,1,0:T(8,128)} fusion(f32[286,8,512]{2,1,0:T(8,128)S(1)} %add_add_fusion, f32[]{:T(128)} %bitcast.203, f32[]{:T(128)} %bitcast.202, f32[]{:T(128)} %bitcast.201, f32[]{:T(128)} %bitcast.200, f32[]{:T(128)} %bitcast.199, f32[]{:T(128)} %bitcast.198, f32[]{:T(128)} %bitcast.197, f32[]{:T(128)} %bitcast.196, f32[]{:T(128)} %bitcast.195, ...), kind=kLoop, calls=%fused_computation.22 | loop fusion | flops 32505856 | bytes 71303232 | tf_op jit(solution)/shard_map/add | solution.py:101
  790.8 8.0 copy.63
  799.0 63.9 %add_convert_fusion = bf16[256,4096]{1,0:T(8,128)(2,1)} fusion(f32[256,4096]{1,0:T(8,128)} %bitcast.487, f32[256,4096]{1,0:T(8,128)} %bitcast.486, f32[256,4096]{1,0:T(8,128)} %bitcast.485, f32[256,4096]{1,0:T(8,128)} %bitcast.484, f32[256,4096]{1,0:T(8,128)} %bitcast.483, f32[256,4096]{1,0:T(8,128)} %bitcast.482, f32[256,4096]{1,0:T(8,128)} %bitcast.481, ...), kind=kLoop, calls=%fused_computation.144 | loop fusion | flops 69206016 | bytes 203578368 | tf_op jit(solution)/shard_map/convert_element_type | solution.py:161
  (254 shorter events, 334.9 us)
Async XLA Ops:
  0.6 16.0 %copy-start.61 = (f32[32]{0:T(128)S(1)}, f32[32]{0:T(128)}, u32[]{:S(2)}) copy-start(f32[32]{0:T(128)} %param.13) | copy-start | bytes 388
  0.6 15.8 %copy-start.57 = (s32[32]{0:T(128)S(1)}, s32[32]{0:T(128)}, u32[]{:S(2)}) copy-start(s32[32]{0:T(128)} %param.11) | copy-start | bytes 388
  0.7 15.8 %copy-start.60 = (f32[32]{0:T(128)S(1)}, f32[32]{0:T(128)}, u32[]{:S(2)}) copy-start(f32[32]{0:T(128)} %param.12) | copy-start | bytes 388
  0.7 15.8 %copy-start.58 = (f32[1,3,6]{2,0,1:T(1,128)S(1)}, f32[1,3,6]{2,0,1:T(1,128)}, u32[]{:S(2)}) copy-start(f32[1,3,6]{2,0,1:T(1,128)} %param.15) | copy-start | bytes 220
  3.1 44.0 %all-to-all-start.2 = ((bf16[16,3,1]{1,2,0:T(2,128)(2,1)}), bf16[16,3,1]{1,2,0:T(2,128)(2,1)S(1)}, u32[]{:S(2)}, u32[]{:S(2)}) async-start(bf16[16,3,1]{1,2,0:T(2,128)(2,1)} %convert_element_type.1294), calls=%async_computation.2 | async-start | bytes 16384 | tf_op jit(solution)/shard_map/all_to_all | solution.py:132
  16.6 37.2 %copy-start.62 = (f32[3]{0:T(128)S(1)}, f32[3]{0:T(128)}, u32[]{:S(2)}) copy-start(f32[3]{0:T(128)} %param.14) | copy-start | bytes 40
  47.2 13.0 %all-to-all-start = ((s32[16,3,1]{1,2,0:T(1,128)}), s32[16,3,1]{1,2,0:T(1,128)S(1)}, u32[]{:S(2)}, u32[]{:S(2)}) async-start(s32[16,3,1]{1,2,0:T(1,128)} %bitcast.8), calls=%async_computation | async-start | bytes 16384 | tf_op jit(solution)/shard_map/all_to_all | solution.py:131
  60.1 145.2 %all-to-all-start.1 = ((bf16[48,8,4096]{2,1,0:T(8,128)(2,1)}), bf16[48,8,4096]{2,1,0:T(8,128)(2,1)S(1)}, u32[]{:S(2)}, u32[]{:S(2)}) async-start(bf16[48,8,4096]{2,1,0:T(8,128)(2,1)} %copy.23), calls=%async_computation.1 | async-start | bytes 6291456 | tf_op jit(solution)/shard_map/all_to_all | solution.py:130
  210.5 51.8 %collective-permute-start = (bf16[15,4096]{1,0:T(8,128)(2,1)S(1)}, bf16[15,4096]{1,0:T(8,128)(2,1)S(1)}, u32[]{:S(2)}, u32[]{:S(2)}) collective-permute-start(bf16[15,4096]{1,0:T(8,128)(2,1)S(1)} %get-tuple-element.58), channel_id=1, source_target_pairs={{0,1},{1,2},{2,3},{3,4},{4,5},{5,6},{6,7},{7,8},{8,9},{9,10},{10,1... | collective-permute-start | bytes 368648 | tf_op jit(solution)/shard_map/ppermute | solution.py:21
  255.2 8.9 %collective-permute-start.1 = (bf16[15,4096]{1,0:T(8,128)(2,1)S(1)}, bf16[15,4096]{1,0:T(8,128)(2,1)S(1)}, u32[]{:S(2)}, u32[]{:S(2)}) collective-permute-start(bf16[15,4096]{1,0:T(8,128)(2,1)S(1)} %get-tuple-element.57), channel_id=1, source_target_pairs={{1,0},{2,1},{3,2},{4,3},{5,4},{6,5},{7,6},{8,7},{9,8},{10,9},{11,1... | collective-permute-start | bytes 368648 | tf_op jit(solution)/shard_map/ppermute | solution.py:24
  265.0 35.2 %copy-start.39 = (bf16[286,7,512]{2,1,0:T(8,128)(2,1)}, bf16[286,7,512]{2,1,0:T(8,128)(2,1)S(1)}, u32[]{:S(2)}) copy-start(bf16[286,7,512]{2,1,0:T(8,128)(2,1)S(1)} %get-tuple-element.55) | copy-start | bytes 6150148
  320.9 8.2 copy-start.21
  335.0 41.7 %slice-start.4 = ((s8[4685824]{0:T(1024)(128)(4,1)}), s8[4194304]{0:T(1024)(128)(4,1)S(1)}, s32[]{:S(2)}) async-start(s8[4685824]{0:T(1024)(128)(4,1)} %bitcast.553), calls=%async_computation.7 | async-start | bytes 8388608
  352.8 23.9 %slice-start.5 = ((s8[4685824]{0:T(1024)(128)(4,1)}), s8[491520]{0:T(1024)(128)(4,1)S(1)}, s32[]{:S(2)}) async-start(s8[4685824]{0:T(1024)(128)(4,1)} %bitcast.553), calls=%async_computation.8 | async-start | bytes 983040
  359.1 17.6 %slice-start.2 = ((s8[4685824]{0:T(1024)(128)(4,1)}), s8[4194304]{0:T(1024)(128)(4,1)S(1)}, s32[]{:S(2)}) async-start(s8[4685824]{0:T(1024)(128)(4,1)} %bitcast.551), calls=%async_computation.5 | async-start | bytes 8388608
  364.9 11.8 %slice-start.3 = ((s8[4685824]{0:T(1024)(128)(4,1)}), s8[491520]{0:T(1024)(128)(4,1)S(1)}, s32[]{:S(2)}) async-start(s8[4685824]{0:T(1024)(128)(4,1)} %bitcast.551), calls=%async_computation.6 | async-start | bytes 983040
  602.1 8.2 slice-start
  602.1 8.2 slice-start.1
  630.1 8.2 copy-start.41
  665.4 8.2 copy-start.23
  790.7 8.2 copy-start.46
  790.7 8.2 copy-start.47
  790.7 8.2 copy-start.48
  790.7 8.2 copy-start.49
  (51 other events, 335.8 us)
where the time goes:
time: 873 us; the launch traced here: 863 us
  local copies, waits for them, and re-layouts  326 us (37%)
  other arithmetic  262 us (30%)
  blocking collectives  98.6 us (11%)
  matrix products  84.4 us (10%)
  between operations  60.6 us (7%)
  starting transfers between devices  27.9 us (3%)
    unnamed x193, local copies, waits for them, and re-layouts  306 us
    mul x6, other arithmetic, row_convolve(): taps_row[tap_index] * rimmed[tap_index:tap_index + row_count]  119 us
    psum x1, blocking collectives, spread(): return lax.psum(jnp.where(mine, value, jnp.zeros_like(value)), axis)  98.6 us
    convert_element_type x1, other arithmetic, shards(): return (matched.astype(jnp.bfloat16), coverage)  63.9 us
    add x3, other arithmetic, row_convolve(): result + taps_row[tap_index] * rimmed[tap_index:tap_index + row_count]  58.9 us
    dot_general x1, matrix products, shards(): jnp.einsum('ib,brw->irw', select_bf, weighted, preferred_element_type=jnp...  29.8 us
    dot_general x3, matrix products, column_convolve(): jnp.einsum('rna,ab->rnb', tiles, band_table(taps_row, 0), preferred_eleme...  17.8 us
  transfers between devices with their start and end apart: 5, of which 2 were waited for; matrix products, arithmetic and copies ran while one was open for 8% of the time, Pallas kernels for 0%

commit v1 on v0

v1 whole, which is shorter than its diff:
```python
import functools

import jax
import jax.numpy as jnp
from jax import lax
from jax.experimental import pallas as pl
from jax.experimental.pallas import tpu as pltpu
from jax.sharding import PartitionSpec as P

MESH = pl.DeviceIdType.MESH
TAPS = 31
HALF = 15
BASES = 3
NPOLY = 6
COLS = 4096
CHUNKS = 8
WIDTH = COLS // CHUNKS
TILES = WIDTH // 128
BLOCKS = 32
ROWS = 256
PEERS = 16
GROUPS = 8
RANKS = 3
SLOTS = RANKS * PEERS
PACKED = SLOTS * 8
EDGE = 16
ALL_ROWS = ROWS * PEERS * GROUPS
FIT_LANE = 2
F32 = jnp.float32
BF16 = jnp.bfloat16


def iota(shape, dim):
    return lax.broadcasted_iota(jnp.int32, shape, dim)


def gaussian(distance, width, norm):
    value = jnp.exp(-(distance * distance) / (2.0 * width * width)) / norm
    return jnp.where(jnp.abs(distance) <= HALF, value, 0.0)


def kernel(
    coef_ref, offset_ref, width_ref, owner_ref, rows_ref, exposure_ref, out_ref, cover_ref,
    padded, weighted, packed, arrived, meta_out, meta_in, fit_out, fit_in, edges,
    pack_mat, row_mat, edge_mat, band_mat, rowconv, y_cols, edge_scale, fit_sum,
    load_sem, fit_send, fit_recv, meta_send, meta_recv, bulk_send, bulk_recv, edge_send, edge_recv,
):
    det = lax.axis_index("det")
    pat = lax.axis_index("patch")
    dev = det * PEERS + pat
    after = lax.rem(dev + 1, PEERS * GROUPS)
    before = lax.rem(dev + PEERS * GROUPS - 1, PEERS * GROUPS)
    after_id = (after // PEERS, lax.rem(after, PEERS))
    before_id = (before // PEERS, lax.rem(before, PEERS))

    barrier = pltpu.get_barrier_semaphore()

    @pl.loop(1, PEERS)
    def _(step):
        pl.semaphore_signal(
            barrier, inc=1, device_id=(det, lax.rem(pat + step, PEERS)), device_id_type=MESH
        )

    @pl.loop(1, GROUPS)
    def _(step):
        pl.semaphore_signal(
            barrier, inc=1, device_id=(lax.rem(det + step, GROUPS), pat), device_id_type=MESH
        )

    pl.semaphore_signal(barrier, inc=1, device_id=after_id, device_id_type=MESH)
    pl.semaphore_signal(barrier, inc=1, device_id=before_id, device_id_type=MESH)

    load = pltpu.make_async_copy(exposure_ref, padded.at[:, :, 128 : 128 + COLS], load_sem)
    load.start()
    padded[:, :, 0:128] = jnp.zeros((BLOCKS, 8, 128), BF16)
    padded[:, :, 128 + COLS :] = jnp.zeros((BLOCKS, 8, 128), BF16)

    peer = rows_ref[0:1, :]
    slot = rows_ref[1:2, :]
    weight = rows_ref[2:3, :]
    fit_row = rows_ref[3:4, 0:128]
    lane = iota((1, ROWS), 1)
    phase = lax.rem(lane, 8).astype(F32)
    row_i = iota((ROWS, ROWS), 0)
    col_i = iota((ROWS, ROWS), 1)
    peer_col = jnp.sum(jnp.where(row_i == col_i, peer, 0.0), axis=1, keepdims=True)
    earlier = (row_i // 8) < (col_i // 8)
    same = jnp.where(jnp.logical_and(peer_col == peer, earlier), 1.0, 0.0)
    rank = jnp.sum(same, axis=0, keepdims=True) * 0.125
    target = rank * 128.0 + peer * 8.0 + phase
    select = jnp.where(iota((PACKED, ROWS), 0).astype(F32) == target, 1.0, 0.0)
    pack_mat[...] = select.astype(BF16)
    row_col = jnp.sum(select * (slot * 8.0 + phase + 1.0), axis=1, keepdims=True)
    weight_col = jnp.sum(select * weight, axis=1, keepdims=True)

    mine = jnp.where(owner_ref[0] == dev, 1.0, 0.0)
    fit_out[...] = jnp.broadcast_to(jnp.where(mine > 0.5, fit_row, 0.0), (8, 128))
    fit_in[det] = fit_out[...]

    pl.semaphore_wait(barrier, PEERS - 1 + GROUPS - 1 + 2)

    @pl.loop(1, GROUPS)
    def _(step):
        pltpu.make_async_remote_copy(
            fit_out, fit_in.at[det], fit_send, fit_recv,
            device_id=(lax.rem(det + step, GROUPS), pat), device_id_type=MESH,
        ).start()

    load.wait()

    def resample(chunk):
        start = pl.multiple_of(chunk * WIDTH, 128)

        @pl.loop(0, BLOCKS)
        def _(block):
            source = padded[block, :, pl.ds(start, WIDTH + 256)].astype(F32)
            offset = offset_ref[block]
            turn = lax.rem(128 - offset, 128)
            ahead = offset >= 0
            lanes = iota((8, 128), 1)
            moved = lanes + offset
            wraps = jnp.logical_or(moved < 0, moved >= 128)
            turned = [
                pltpu.roll(source[:, t * 128 : (t + 1) * 128], turn, axis=1)
                for t in range(TILES + 2)
            ]
            shifted = []
            for t in range(TILES + 2):
                right = turned[min(t + 1, TILES + 1)]
                left = turned[max(t - 1, 0)]
                shifted.append(jnp.where(wraps, jnp.where(ahead, right, left), turned[t]))
            coefs = [coef_ref[block * 6 + i] for i in range(6)]
            total = [coefs[2] * shifted[t] for t in range(1, TILES + 1)]
            for tap in (-2, -1, 1, 2, 3):
                rolled = [pltpu.roll(value, (128 - tap) % 128, axis=1) for value in shifted]
                for t in range(1, TILES + 1):
                    if tap > 0:
                        value = jnp.where(lanes < 128 - tap, rolled[t], rolled[t + 1])
                    else:
                        value = jnp.where(lanes >= -tap, rolled[t], rolled[t - 1])
                    total[t - 1] = total[t - 1] + coefs[tap + 2] * value
            weighted[block] = jnp.concatenate(total, axis=1).astype(BF16)

        gathered = jnp.dot(
            pack_mat[...], weighted[...].reshape(ROWS, WIDTH), preferred_element_type=F32
        )
        packed[chunk] = gathered.astype(BF16).reshape(RANKS, PEERS, 8, WIDTH)

    def send(chunk):
        pltpu.make_async_copy(
            packed.at[chunk, :, pat], arrived.at[chunk, 0:RANKS, pat], bulk_recv.at[chunk]
        ).start()

        @pl.loop(1, PEERS)
        def _(step):
            other = lax.rem(pat + step, PEERS)
            pltpu.make_async_remote_copy(
                packed.at[chunk, :, other], arrived.at[chunk, 0:RANKS, pat],
                bulk_send.at[chunk], bulk_recv.at[chunk],
                device_id=(det, other), device_id_type=MESH,
            ).start()

    resample(0)
    whole = fit_in.at[0 : GROUPS - 1]
    pltpu.make_async_copy(whole, whole, fit_recv).wait()
    chosen = jnp.sum(fit_in[...], axis=0)
    lanes_m = iota((PACKED, 128), 1)
    meta = jnp.where(lanes_m == 0, row_col, jnp.where(lanes_m == 1, weight_col, chosen[0:1, :]))
    meta_out[...] = meta.reshape(RANKS, PEERS, 8, 128)
    pltpu.make_async_copy(meta_out.at[:, pat], meta_in.at[:, pat], meta_recv).start()

    @pl.loop(1, PEERS)
    def _(step):
        other = lax.rem(pat + step, PEERS)
        pltpu.make_async_remote_copy(
            meta_out.at[:, other], meta_in.at[:, pat], meta_send, meta_recv,
            device_id=(det, other), device_id_type=MESH,
        ).start()

    send(0)

    @pl.loop(1, CHUNKS)
    def _(chunk):
        resample(chunk)
        send(chunk)

    span = iota((8, 128), 1).astype(F32) - HALF
    norms = []
    for k in range(BASES):
        value = jnp.exp(-(span * span) / (2.0 * width_ref[k] * width_ref[k]))
        value = jnp.where(span <= HALF, value, 0.0)
        norms.append(jnp.sum(value, axis=1, keepdims=True)[0:1, :])
    across = (iota((512, 256), 0) - 128 - iota((512, 256), 1)).astype(F32)
    for k in range(BASES):
        band_mat[k] = gaussian(across, width_ref[k], norms[k]).astype(BF16)
    y_cols[...] = 2.0 * (dev * ROWS + iota((ROWS, 128), 0)).astype(F32) / (ALL_ROWS - 1) - 1.0
    for k in range(BASES):
        rowconv[k, :, 0:128] = jnp.zeros((ROWS, 128), BF16)
        rowconv[k, :, 128 + COLS :] = jnp.zeros((ROWS, 128), BF16)

    pltpu.make_async_copy(meta_in, meta_in, meta_recv).wait()
    meta_got = meta_in[...].reshape(PACKED, 128)
    got_row = meta_got[:, 0:1] - 1.0
    got_weight = meta_got[:, 1:2]
    lands = jnp.where(got_row == iota((PACKED, ROWS), 1).astype(F32), 1.0, 0.0)
    cover = jnp.sum(lands * got_weight, axis=0, keepdims=True)
    cover_ref[...] = jnp.broadcast_to(cover, (8, ROWS))
    scale = 1.0 / jnp.maximum(cover, 1.0)
    fit_sum[...] = jnp.sum(meta_in[0], axis=0)
    lands = lands.astype(BF16)
    contract = (((1,), (1,)), ((), ()))
    reach = (iota((ROWS, ROWS), 1) - iota((ROWS, ROWS), 0)).astype(F32)
    rim = iota((ROWS, 2 * EDGE), 1)
    rim_at = jnp.where(rim < EDGE, rim - EDGE, rim + ROWS - EDGE)
    rim_reach = (rim_at - iota((ROWS, 2 * EDGE), 0)).astype(F32)
    low_live = jnp.where(dev > 0, 1.0, 0.0)
    high_live = jnp.where(dev < PEERS * GROUPS - 1, 1.0, 0.0)
    rim_live = jnp.where(rim < EDGE, low_live, high_live)
    for k in range(BASES):
        inner = (gaussian(reach, width_ref[k], norms[k]) * scale).astype(BF16)
        spread = lax.dot_general(inner, lands, contract, preferred_element_type=F32)
        row_mat[k * ROWS : (k + 1) * ROWS, 0:PACKED] = spread.astype(BF16)
        outer = gaussian(rim_reach, width_ref[k], norms[k]) * rim_live
        row_mat[k * ROWS : (k + 1) * ROWS, PACKED:] = outer.astype(BF16)
    edge_i = iota((2 * EDGE, ROWS), 0)
    edge_row = jnp.where(edge_i < EDGE, edge_i, edge_i + ROWS - 2 * EDGE)
    picks = jnp.where(edge_row == iota((2 * EDGE, ROWS), 1), 1.0, 0.0)
    edge_mat[...] = lax.dot_general(
        picks.astype(BF16), lands, contract, preferred_element_type=F32
    ).astype(BF16)
    edge_scale[...] = jnp.broadcast_to(
        jnp.sum(picks * scale, axis=1, keepdims=True), (2 * EDGE, 128)
    )

    def edge_copies(chunk):
        return (
            pltpu.make_async_remote_copy(
                edges.at[chunk, 0:2], arrived.at[chunk, RANKS, 2:4],
                edge_send.at[chunk], edge_recv.at[chunk],
                device_id=before_id, device_id_type=MESH,
            ),
            pltpu.make_async_remote_copy(
                edges.at[chunk, 2:4], arrived.at[chunk, RANKS, 0:2],
                edge_send.at[chunk], edge_recv.at[chunk],
                device_id=after_id, device_id_type=MESH,
            ),
        )

    def make_edges(chunk):
        landed = arrived.at[chunk, 0:RANKS]
        pltpu.make_async_copy(landed, landed, bulk_recv.at[chunk]).wait()
        rows = jnp.dot(
            edge_mat[...], arrived[chunk, 0:RANKS].reshape(PACKED, WIDTH),
            preferred_element_type=F32,
        )
        rows = rows * edge_scale[:, 0:1]
        edges[chunk] = rows.astype(BF16).reshape(4, 8, WIDTH)
        for copy in edge_copies(chunk):
            copy.start()

    def row_stage(chunk):
        rims = arrived.at[chunk, RANKS, 0:4]
        pltpu.make_async_copy(rims, rims, edge_recv.at[chunk]).wait()
        got = arrived[chunk, 0:RANKS].reshape(PACKED, WIDTH)
        rim_rows = arrived[chunk, RANKS, 0:4].reshape(2 * EDGE, WIDTH)
        full = jnp.concatenate([got, rim_rows], axis=0)
        at = pl.ds(pl.multiple_of(128 + chunk * WIDTH, 128), WIDTH)
        for k in range(BASES):
            value = jnp.dot(
                row_mat[k * ROWS : (k + 1) * ROWS, :], full, preferred_element_type=F32
            )
            rowconv[k, :, at] = value.astype(BF16)

    fit_now = fit_sum[0:1, :]
    terms = [
        [
            jnp.sum(
                jnp.where(iota((1, 128), 1) == FIT_LANE + k * NPOLY + i, fit_now, 0.0),
                axis=1, keepdims=True,
            )
            for i in range(NPOLY)
        ]
        for k in range(BASES)
    ]

    def col_tile(tile):
        at = pl.multiple_of(tile * 256, 128)
        x = 2.0 * (tile * 256 + iota((1, 256), 1)).astype(F32) / (COLS - 1) - 1.0
        y = y_cols[:, 0:1]
        result = None
        for k in range(BASES):
            value = jnp.dot(
                rowconv[k, :, pl.ds(at, 512)], band_mat[k], preferred_element_type=F32
            )
            a = terms[k]
            level = a[0] + a[1] * x + a[3] * x * x
            slope = a[2] + a[4] * x
            field = level + y * slope + (a[5] * y) * y
            part = field * value
            result = part if result is None else result + part
        out_ref[:, pl.ds(at, 256)] = result.astype(BF16)

    make_edges(0)

    @pl.loop(1, CHUNKS)
    def _(chunk):
        make_edges(chunk)
        row_stage(chunk - 1)

        @pl.when(chunk > 1)
        def _():
            col_tile(2 * chunk - 3)

        col_tile(2 * chunk - 2)

    row_stage(CHUNKS - 1)
    for tile in (2 * CHUNKS - 3, 2 * CHUNKS - 2, 2 * CHUNKS - 1):
        col_tile(tile)

    pltpu.make_async_copy(whole, whole, fit_send).wait()
    sent = meta_out.at[:, 0 : PEERS - 1]
    pltpu.make_async_copy(sent, sent, meta_send).wait()

    @pl.loop(0, CHUNKS)
    def _(chunk):
        gone = packed.at[chunk, :, 0 : PEERS - 1]
        pltpu.make_async_copy(gone, gone, bulk_send.at[chunk]).wait()
        pltpu.make_async_copy(edges.at[chunk], edges.at[chunk], edge_send.at[chunk]).wait()


def shards(
    exposure, block_dest, band_offset, col_shift, block_weight, basis_width, kernel_fit, fit_owner
):
    positions = jnp.arange(-2, 4).astype(F32)[None, :] - col_shift[:, None]
    coefs = jnp.sinc(positions) * jnp.sinc(positions / 3.0) * block_weight[:, None]
    fit_row = jnp.pad(kernel_fit.reshape(1, BASES * NPOLY), ((0, 0), (FIT_LANE, ROWS - FIT_LANE - BASES * NPOLY)))
    peer = block_dest // BLOCKS % PEERS
    slot = block_dest % BLOCKS
    table = jnp.stack([peer.astype(F32), slot.astype(F32), block_weight])
    rows = jnp.concatenate(
        [jnp.repeat(table, 8, axis=1), fit_row, jnp.zeros((4, ROWS), F32)], axis=0
    )
    smem = pl.BlockSpec(memory_space=pltpu.SMEM)
    vmem = pl.BlockSpec(memory_space=pltpu.VMEM)
    matched, cover = pl.pallas_call(
        kernel,
        out_shape=(
            jax.ShapeDtypeStruct((ROWS, COLS), BF16),
            jax.ShapeDtypeStruct((8, ROWS), F32),
        ),
        in_specs=[smem, smem, smem, smem, vmem, pl.BlockSpec(memory_space=pl.ANY)],
        out_specs=(vmem, vmem),
        scratch_shapes=[
            pltpu.VMEM((BLOCKS, 8, COLS + 256), BF16),
            pltpu.VMEM((BLOCKS, 8, WIDTH), BF16),
            pltpu.VMEM((CHUNKS, RANKS, PEERS, 8, WIDTH), BF16),
            pltpu.VMEM((CHUNKS, RANKS + 1, PEERS, 8, WIDTH), BF16),
            pltpu.VMEM((RANKS, PEERS, 8, 128), F32),
            pltpu.VMEM((RANKS, PEERS, 8, 128), F32),
            pltpu.VMEM((8, 128), F32),
            pltpu.VMEM((GROUPS, 8, 128), F32),
            pltpu.VMEM((CHUNKS, 4, 8, WIDTH), BF16),
            pltpu.VMEM((PACKED, ROWS), BF16),
            pltpu.VMEM((BASES * ROWS, PACKED + 2 * EDGE), BF16),
            pltpu.VMEM((2 * EDGE, PACKED), BF16),
            pltpu.VMEM((BASES, 512, 256), BF16),
            pltpu.VMEM((BASES, ROWS, COLS + 256), BF16),
            pltpu.VMEM((ROWS, 128), F32),
            pltpu.VMEM((2 * EDGE, 128), F32),
            pltpu.VMEM((8, 128), F32),
            pltpu.SemaphoreType.DMA,
            pltpu.SemaphoreType.DMA,
            pltpu.SemaphoreType.DMA,
            pltpu.SemaphoreType.DMA,
            pltpu.SemaphoreType.DMA,
            pltpu.SemaphoreType.DMA((CHUNKS,)),
            pltpu.SemaphoreType.DMA((CHUNKS,)),
            pltpu.SemaphoreType.DMA((CHUNKS,)),
            pltpu.SemaphoreType.DMA((CHUNKS,)),
        ],
        compiler_params=pltpu.CompilerParams(
            collective_id=0, has_side_effects=True, vmem_limit_bytes=52 << 20
        ),
        name="coadd_match",
    )(
        coefs.reshape(-1), band_offset, basis_width, fit_owner, rows,
        exposure.reshape(BLOCKS, 8, COLS),
    )
    return matched, cover[0].reshape(BLOCKS, 8)[:, 0]


def solution(mesh):
    row_spec = P(("det", "patch"))
    in_specs = (
        P(("det", "patch"), None), row_spec, row_spec, row_spec, row_spec,
        P(), P(("det", "patch"), None, None), P(),
    )
    out_specs = (P(("det", "patch"), None), row_spec)
    return jax.shard_map(shards, mesh=mesh, in_specs=in_specs, out_specs=out_specs, check_vma=False)
```

time: 873 us -> 96 us (0.11)
  the two profiles are of different devices: /device:TPU:1 before, /device:TPU:0 now
where the time goes in v1:
time: 96 us; the launch traced here: 95.8 us
  Pallas kernels  85.9 us (89%)
  local copies, waits for them, and re-layouts  5.63 us (6%)
  other arithmetic  2.9 us (3%)
  between operations  1.31 us (1%)
    pallas_call x1, Pallas kernels, shards(): pl.pallas_call(kernel, out_shape=(jax.ShapeDtypeStruct((ROWS, COLS), BF16...  85.9 us
    unnamed x5, local copies, waits for them, and re-layouts  4.45 us

profile of v1, /device:TPU:0, one launch (start us, length us, event | category | flops | bytes accessed | tf_op | source)
XLA Modules:
  0.0 95.8 jit_solution(2245946308815469669)
XLA Ops:
  1.3 0.1 pad.7.clone
  1.4 0.7 fusion.47
  2.0 0.7 pad_maximum_fusion
  2.7 0.7 reduce
  3.4 0.1 reshape.25
  3.5 0.8 fusion.14
  4.3 0.1 reshape.23.coef_ref
  4.4 0.1 broadcast_in_dim.12
  4.5 0.1 reshape.24
  4.6 0.1 fusion.44.rows_ref
  4.6 0.0 copy-start
  4.6 0.7 copy-done
  5.3 0.0 copy-start.1
  5.3 0.7 copy-done.1
  6.0 85.9 %coadd_match.1 = (bf16[256,4096]{1,0:T(8,128)(2,1)}, f32[8,256]{1,0:T(8,128)S(1)}) custom-call(f32[192]{0:T(256)S(1)} %reshape.23.coef_ref, s32[32]{0:T(128)S(1)} %copy-done, f32[3]{0:T(128)S(1)} %copy-done.1, s32[1]{0:T(128)S(6)} %copy.12.owner_ref, f32[8,256]{1,0:T(8,128)S(1)} %fusion.44.rows_ref, bf16[32,8,4096]{2,1,0:T(8,128)(2,1)} %bitcast.6), custom_call_target="tpu_custom_call" | custom-call | tf_op jit(solution)/shard_map/coadd_match/pallas_call | solution.py:345
  91.9 0.1 reshape_squeeze.3
  92.0 0.6 slice_reduce_fusion
  92.7 3.1 %copy.13 = bf16[256,4096]{1,0:T(8,128)(2,1)} copy(bf16[256,4096]{1,0:T(8,128)(2,1)} %get-tuple-element.11) | data formatting | bytes 4194304
  (3 shorter events, 0.0 us)
Async XLA Ops:
  4.6 0.7 copy-start
  5.3 0.7 copy-start.1

commit v2 on v1

v2 whole, which is shorter than its diff:
```python
import functools

import jax
import jax.numpy as jnp
from jax import lax
from jax.experimental import pallas as pl
from jax.experimental.pallas import tpu as pltpu
from jax.sharding import PartitionSpec as P

MESH = pl.DeviceIdType.MESH
TAPS = 31
HALF = 15
BASES = 3
NPOLY = 6
COLS = 4096
CHUNKS = 8
WINDOW = 3
UNROLL = 16
LEAD = 9
LAG = 2
WIDTH = COLS // CHUNKS
TILES = WIDTH // 128
BLOCKS = 32
ROWS = 256
PEERS = 16
GROUPS = 8
RANKS = 3
SLOTS = RANKS * PEERS
PACKED = SLOTS * 8
EDGE = 16
ALL_ROWS = ROWS * PEERS * GROUPS
FIT_LANE = 6
F32 = jnp.float32
BF16 = jnp.bfloat16


def iota(shape, dim):
    return lax.broadcasted_iota(jnp.int32, shape, dim)


def sinc(value):
    angle = jnp.pi * value
    return jnp.where(value == 0.0, 1.0, jnp.sin(angle) / jnp.where(value == 0.0, 1.0, angle))


def gaussian(distance, width, norm):
    value = jnp.exp(-(distance * distance) / (2.0 * width * width)) / norm
    return jnp.where(jnp.abs(distance) <= HALF, value, 0.0)


def kernel(
    dest_hbm, offset_hbm, shift_hbm, weight_hbm, width_hbm, fit_hbm, owner_ref, exposure_ref,
    out_ref, cover_ref,
    dest_ref, offset_ref, shift_ref, weight_ref, width_ref, fit_ref, small_sem,
    padded, weighted, packed, arrived, meta_out, meta_in, fit_out, fit_in, edges,
    pack_mat, row_mat, edge_mat, band_mat, rowconv, y_cols, edge_scale, coef_table, coef_ref,
    moved, shift_mat, coef_wide,
    load_sem, coef_sem, fit_send, fit_recv, meta_send, meta_recv, bulk_send, bulk_recv, edge_send, edge_recv,
):
    det = lax.axis_index("det")
    pat = lax.axis_index("patch")
    dev = det * PEERS + pat
    after = lax.rem(dev + 1, PEERS * GROUPS)
    before = lax.rem(dev + PEERS * GROUPS - 1, PEERS * GROUPS)
    after_id = (after // PEERS, lax.rem(after, PEERS))
    before_id = (before // PEERS, lax.rem(before, PEERS))

    load = pltpu.make_async_copy(exposure_ref, padded.at[:, :, 128 : 128 + COLS], load_sem)
    load.start()
    smalls = [
        pltpu.make_async_copy(source, target, small_sem.at[i])
        for i, (source, target) in enumerate(
            (
                (dest_hbm, dest_ref), (shift_hbm, shift_ref), (weight_hbm, weight_ref),
                (fit_hbm, fit_ref), (offset_hbm, offset_ref),
                (width_hbm, width_ref),
            )
        )
    ]
    for copy in smalls:
        copy.start()

    barrier = pltpu.get_barrier_semaphore()

    @pl.loop(1, PEERS)
    def _(step):
        pl.semaphore_signal(
            barrier, inc=1, device_id=(det, lax.rem(pat + step, PEERS)), device_id_type=MESH
        )

    @pl.loop(1, GROUPS)
    def _(step):
        pl.semaphore_signal(
            barrier, inc=1, device_id=(lax.rem(det + step, GROUPS), pat), device_id_type=MESH
        )

    pl.semaphore_signal(barrier, inc=1, device_id=after_id, device_id_type=MESH)
    pl.semaphore_signal(barrier, inc=1, device_id=before_id, device_id_type=MESH)

    padded[:, :, 0:128] = jnp.zeros((BLOCKS, 8, 128), BF16)
    padded[:, :, 128 + COLS :] = jnp.zeros((BLOCKS, 8, 128), BF16)

    for copy in smalls:
        copy.wait()

    deep = iota((BLOCKS, 128), 0)
    shift = jnp.zeros((BLOCKS, 128), F32)
    heavy = jnp.zeros((BLOCKS, 128), F32)
    for b in range(BLOCKS):
        shift = jnp.where(deep == b, shift_ref[b], shift)
        heavy = jnp.where(deep == b, weight_ref[b], heavy)
    position = (iota((BLOCKS, 128), 1) - 2).astype(F32) - shift
    coef_table[...] = sinc(position) * sinc(position / 3.0) * heavy
    coef_copy = pltpu.make_async_copy(coef_table, coef_ref, coef_sem)
    coef_copy.start()

    mine = jnp.where(owner_ref[0] == dev, 1.0, 0.0)
    lane_1 = iota((8, 128), 1)
    fit_row = jnp.zeros((8, 128), F32)
    for k in range(BASES):
        for n in range(NPOLY):
            fit_row = jnp.where(lane_1 == FIT_LANE + k * NPOLY + n, fit_ref[k, 0, n], fit_row)
    fit_row = jnp.where(mine > 0.5, fit_row, 0.0)
    fit_out[...] = fit_row
    fit_in[det] = fit_row

    lane = iota((1, ROWS), 1)
    owner_block = lane // 8
    phase = lax.rem(lane, 8)
    peer = jnp.zeros((1, ROWS), jnp.int32)
    slot = jnp.zeros((1, ROWS), jnp.int32)
    weight = jnp.zeros((1, ROWS), F32)
    for b in range(BLOCKS):
        here = owner_block == b
        goal = dest_ref[b]
        peer = jnp.where(here, (goal >> 5) & (PEERS - 1), peer)
        slot = jnp.where(here, goal & (BLOCKS - 1), slot)
        weight = jnp.where(here, weight_ref[b], weight)
    rank = jnp.zeros((1, ROWS), jnp.int32)
    for b in range(BLOCKS - 1):
        to = (dest_ref[b] >> 5) & (PEERS - 1)
        rank = rank + jnp.where(jnp.logical_and(peer == to, owner_block > b), 1, 0)
    target = rank * 128 + peer * 8 + phase
    select = jnp.where(iota((PACKED, ROWS), 0) == target, 1.0, 0.0)
    pack_mat[...] = select.astype(BF16)
    row_value = (slot * 8 + phase + 1).astype(F32)
    row_col = jnp.sum(select * row_value, axis=1, keepdims=True)
    weight_col = jnp.sum(select * weight, axis=1, keepdims=True)


    def resample(chunk):
        start = pl.multiple_of(chunk * WIDTH, 128)

        def one(block):
            source = padded[block, :, pl.ds(start, WIDTH + 256)].astype(F32)
            turn = LEAD - offset_ref[block]
            carried = iota((8, 128), 1) < turn
            turned = [
                pltpu.roll(source[:, t * 128 : (t + 1) * 128], turn, axis=1)
                for t in range(TILES + 2)
            ]
            parts = [jnp.where(carried, turned[t], turned[t + 1]) for t in range(TILES + 1)]
            return jnp.concatenate(parts, axis=1).astype(BF16)

        @pl.loop(0, BLOCKS // UNROLL)
        def _(group):
            values = [one(group * UNROLL + i) for i in range(UNROLL)]
            for i in range(UNROLL):
                moved[group * UNROLL + i] = values[i]

        for t in range(TILES):
            window = moved[:, :, t * 128 : t * 128 + 256].reshape(ROWS, 256)
            total = None
            for pair in range(3):
                pieces = jnp.dot(
                    window, shift_mat[:, pair * 256 : (pair + 1) * 256],
                    preferred_element_type=F32,
                )
                for side in range(2):
                    part = pieces[:, side * 128 : (side + 1) * 128] * coef_wide[2 * pair + side]
                    total = part if total is None else total + part
            weighted[:, t * 128 : (t + 1) * 128] = total.astype(BF16)

        gathered = jnp.dot(
            pack_mat[...], weighted[...], preferred_element_type=F32
        )
        packed[chunk] = gathered.astype(BF16).reshape(RANKS, PEERS, 8, WIDTH)

    def send(chunk):
        pltpu.make_async_copy(
            packed.at[chunk, :, pat], arrived.at[chunk, 0:RANKS, pat], bulk_recv.at[chunk]
        ).start()

        @pl.loop(1, PEERS)
        def _(step):
            other = lax.rem(pat + step, PEERS)
            pltpu.make_async_remote_copy(
                packed.at[chunk, :, other], arrived.at[chunk, 0:RANKS, pat],
                bulk_send.at[chunk], bulk_recv.at[chunk],
                device_id=(det, other), device_id_type=MESH,
            ).start()

    spot = iota((256, 768), 1)
    reads = lax.rem(spot, 128) + spot // 128 + (LEAD - 2)
    shift_mat[...] = jnp.where(iota((256, 768), 0) == reads, 1.0, 0.0).astype(BF16)
    coef_copy.wait()
    for b in range(BLOCKS):
        for i in range(6):
            coef_wide[i, b * 8 : (b + 1) * 8, :] = jnp.full((8, 128), coef_ref[b, i], F32)
    load.wait()

    resample(0)

    span = iota((8, 128), 1).astype(F32) - HALF
    norms = []
    for k in range(BASES):
        value = jnp.exp(-(span * span) / (2.0 * width_ref[k] * width_ref[k]))
        value = jnp.where(span <= HALF, value, 0.0)
        norms.append(jnp.sum(value, axis=1, keepdims=True)[0:1, :])
    across = (iota((512, 256), 0) - 128 - iota((512, 256), 1)).astype(F32)
    for k in range(BASES):
        band_mat[k] = gaussian(across, width_ref[k], norms[k]).astype(BF16)
    y_cols[...] = 2.0 * (dev * ROWS + iota((ROWS, 128), 0)).astype(F32) / (ALL_ROWS - 1) - 1.0
    for k in range(BASES):
        rowconv[k, :, 0:128] = jnp.zeros((ROWS, 128), BF16)
        rowconv[k, :, 128 + COLS :] = jnp.zeros((ROWS, 128), BF16)

    pl.semaphore_wait(barrier, PEERS - 1 + GROUPS - 1 + 2)

    @pl.loop(1, GROUPS)
    def _(step):
        pltpu.make_async_remote_copy(
            fit_out, fit_in.at[det], fit_send, fit_recv,
            device_id=(lax.rem(det + step, GROUPS), pat), device_id_type=MESH,
        ).start()

    send(0)
    whole = fit_in.at[0 : GROUPS - 1]
    pltpu.make_async_copy(whole, whole, fit_recv).wait()
    chosen = jnp.sum(fit_in[...], axis=0)
    lanes_m = iota((128, 128), 1)
    meta = jnp.broadcast_to(chosen[0:1, :], (128, 128))
    for r in range(RANKS):
        part = slice(r * 128, (r + 1) * 128)
        meta = jnp.where(lanes_m == r, row_col[part], meta)
        meta = jnp.where(lanes_m == RANKS + r, weight_col[part], meta)
    meta_out[...] = meta.reshape(PEERS, 8, 128)
    pltpu.make_async_copy(meta_out.at[pat], meta_in.at[pat], meta_recv).start()

    @pl.loop(1, PEERS)
    def _(step):
        other = lax.rem(pat + step, PEERS)
        pltpu.make_async_remote_copy(
            meta_out.at[other], meta_in.at[pat], meta_send, meta_recv,
            device_id=(det, other), device_id_type=MESH,
        ).start()

    @pl.loop(1, WINDOW)
    def _(chunk):
        resample(chunk)
        send(chunk)

    pltpu.make_async_copy(meta_in, meta_in, meta_recv).wait()
    meta_got = meta_in[...].reshape(128, 128)
    got_row = jnp.concatenate([meta_got[:, r : r + 1] for r in range(RANKS)], axis=0) - 1.0
    got_weight = jnp.concatenate(
        [meta_got[:, RANKS + r : RANKS + r + 1] for r in range(RANKS)], axis=0
    )
    lands = jnp.where(got_row == iota((PACKED, ROWS), 1).astype(F32), 1.0, 0.0)
    cover = jnp.sum(lands * got_weight, axis=0, keepdims=True)
    heads = jnp.where(got_row == (8 * iota((PACKED, 128), 1)).astype(F32), got_weight, 0.0)
    cover_ref[...] = jnp.sum(heads, axis=0, keepdims=True)[:, 0:BLOCKS]
    scale = 1.0 / jnp.maximum(cover, 1.0)
    fit_now = jnp.sum(meta_got, axis=0, keepdims=True) * 0.125
    lands = lands.astype(BF16)
    contract = (((1,), (1,)), ((), ()))
    reach = (iota((ROWS, ROWS), 1) - iota((ROWS, ROWS), 0)).astype(F32)
    rim = iota((ROWS, 2 * EDGE), 1)
    rim_at = jnp.where(rim < EDGE, rim - EDGE, rim + ROWS - EDGE)
    rim_reach = (rim_at - iota((ROWS, 2 * EDGE), 0)).astype(F32)
    low_live = jnp.where(dev > 0, 1.0, 0.0)
    high_live = jnp.where(dev < PEERS * GROUPS - 1, 1.0, 0.0)
    rim_live = jnp.where(rim < EDGE, low_live, high_live)
    for k in range(BASES):
        inner = (gaussian(reach, width_ref[k], norms[k]) * scale).astype(BF16)
        spread = lax.dot_general(inner, lands, contract, preferred_element_type=F32)
        row_mat[k * ROWS : (k + 1) * ROWS, 0:PACKED] = spread.astype(BF16)
        outer = gaussian(rim_reach, width_ref[k], norms[k]) * rim_live
        row_mat[k * ROWS : (k + 1) * ROWS, PACKED:] = outer.astype(BF16)
    edge_i = iota((2 * EDGE, ROWS), 0)
    edge_row = jnp.where(edge_i < EDGE, edge_i, edge_i + ROWS - 2 * EDGE)
    picks = jnp.where(edge_row == iota((2 * EDGE, ROWS), 1), 1.0, 0.0)
    edge_mat[...] = lax.dot_general(
        picks.astype(BF16), lands, contract, preferred_element_type=F32
    ).astype(BF16)
    edge_scale[...] = jnp.broadcast_to(
        jnp.sum(picks * scale, axis=1, keepdims=True), (2 * EDGE, 128)
    )

    def edge_copies(chunk):
        return (
            pltpu.make_async_remote_copy(
                edges.at[chunk, 0:2], arrived.at[chunk, RANKS, 2:4],
                edge_send.at[chunk], edge_recv.at[chunk],
                device_id=before_id, device_id_type=MESH,
            ),
            pltpu.make_async_remote_copy(
                edges.at[chunk, 2:4], arrived.at[chunk, RANKS, 0:2],
                edge_send.at[chunk], edge_recv.at[chunk],
                device_id=after_id, device_id_type=MESH,
            ),
        )

    def wait_bulk(chunk):
        landed = arrived.at[chunk, 0:RANKS]
        pltpu.make_async_copy(landed, landed, bulk_recv.at[chunk]).wait()

    def make_edges(chunk):
        rows = jnp.dot(
            edge_mat[...], arrived[chunk, 0:RANKS].reshape(PACKED, WIDTH),
            preferred_element_type=F32,
        )
        rows = rows * edge_scale[:, 0:1]
        edges[chunk] = rows.astype(BF16).reshape(4, 8, WIDTH)
        for copy in edge_copies(chunk):
            copy.start()

    def row_stage(chunk):
        rims = arrived.at[chunk, RANKS, 0:4]
        pltpu.make_async_copy(rims, rims, edge_recv.at[chunk]).wait()
        got = arrived[chunk, 0:RANKS].reshape(PACKED, WIDTH)
        rim_rows = arrived[chunk, RANKS, 0:4].reshape(2 * EDGE, WIDTH)
        full = jnp.concatenate([got, rim_rows], axis=0)
        at = pl.ds(pl.multiple_of(128 + chunk * WIDTH, 128), WIDTH)
        for k in range(BASES):
            value = jnp.dot(
                row_mat[k * ROWS : (k + 1) * ROWS, :], full, preferred_element_type=F32
            )
            rowconv[k, :, at] = value.astype(BF16)

    terms = [
        [
            jnp.sum(
                jnp.where(iota((1, 128), 1) == FIT_LANE + k * NPOLY + i, fit_now, 0.0),
                axis=1, keepdims=True,
            )
            for i in range(NPOLY)
        ]
        for k in range(BASES)
    ]

    def col_tile(tile):
        at = pl.multiple_of(tile * 256, 128)
        x = 2.0 * (tile * 256 + iota((1, 256), 1)).astype(F32) / (COLS - 1) - 1.0
        y = y_cols[:, 0:1]
        result = None
        for k in range(BASES):
            value = jnp.dot(
                rowconv[k, :, pl.ds(at, 512)], band_mat[k], preferred_element_type=F32
            )
            a = terms[k]
            level = a[0] + a[1] * x + a[3] * x * x
            slope = a[2] + a[4] * x
            field = level + y * slope + (a[5] * y) * y
            part = field * value
            result = part if result is None else result + part
        out_ref[:, pl.ds(at, 256)] = result.astype(BF16)

    @pl.loop(0, CHUNKS)
    def _(chunk):
        @pl.when(chunk + WINDOW < CHUNKS)
        def _():
            resample(chunk + WINDOW)

        wait_bulk(chunk)

        make_edges(chunk)

        @pl.when(chunk + WINDOW < CHUNKS)
        def _():
            send(chunk + WINDOW)

        @pl.when(chunk >= LAG)
        def _():
            row_stage(chunk - LAG)
            col_tile(2 * (chunk - LAG))

        @pl.when(chunk > LAG)
        def _():
            col_tile(2 * (chunk - LAG) - 1)

    for last in range(CHUNKS - LAG, CHUNKS):
        row_stage(last)
        col_tile(2 * last - 1)
        col_tile(2 * last)
    col_tile(2 * CHUNKS - 1)

    pltpu.make_async_copy(whole, whole, fit_send).wait()
    sent = meta_out.at[0 : PEERS - 1]
    pltpu.make_async_copy(sent, sent, meta_send).wait()

    @pl.loop(0, CHUNKS)
    def _(chunk):
        gone = packed.at[chunk, :, 0 : PEERS - 1]
        pltpu.make_async_copy(gone, gone, bulk_send.at[chunk]).wait()
        pltpu.make_async_copy(edges.at[chunk], edges.at[chunk], edge_send.at[chunk]).wait()


def shards(
    exposure, block_dest, band_offset, col_shift, block_weight, basis_width, kernel_fit, fit_owner
):
    hbm = pl.BlockSpec(memory_space=pltpu.HBM)
    smem = pl.BlockSpec(memory_space=pltpu.SMEM)
    in_hbm = functools.partial(pltpu.with_memory_space_constraint, memory_space=pltpu.HBM)
    vmem = pl.BlockSpec(memory_space=pltpu.VMEM)
    matched, cover = pl.pallas_call(
        kernel,
        out_shape=(
            jax.ShapeDtypeStruct((ROWS, COLS), BF16),
            jax.ShapeDtypeStruct((1, BLOCKS), F32),
        ),
        in_specs=[hbm] * 6 + [smem, hbm],
        out_specs=(vmem, vmem),
        scratch_shapes=[
            pltpu.SMEM((BLOCKS,), jnp.int32),
            pltpu.SMEM((BLOCKS,), jnp.int32),
            pltpu.SMEM((BLOCKS,), F32),
            pltpu.SMEM((BLOCKS,), F32),
            pltpu.SMEM((BASES,), F32),
            pltpu.SMEM((BASES, 1, NPOLY), F32),
            pltpu.SemaphoreType.DMA((6,)),
            pltpu.VMEM((BLOCKS, 8, COLS + 256), BF16),
            pltpu.VMEM((ROWS, WIDTH), BF16),
            pltpu.VMEM((CHUNKS, RANKS, PEERS, 8, WIDTH), BF16),
            pltpu.VMEM((CHUNKS, RANKS + 1, PEERS, 8, WIDTH), BF16),
            pltpu.VMEM((PEERS, 8, 128), F32),
            pltpu.VMEM((PEERS, 8, 128), F32),
            pltpu.VMEM((8, 128), F32),
            pltpu.VMEM((GROUPS, 8, 128), F32),
            pltpu.VMEM((CHUNKS, 4, 8, WIDTH), BF16),
            pltpu.VMEM((PACKED, ROWS), BF16),
            pltpu.VMEM((BASES * ROWS, PACKED + 2 * EDGE), BF16),
            pltpu.VMEM((2 * EDGE, PACKED), BF16),
            pltpu.VMEM((BASES, 512, 256), BF16),
            pltpu.VMEM((BASES, ROWS, COLS + 256), BF16),
            pltpu.VMEM((ROWS, 128), F32),
            pltpu.VMEM((2 * EDGE, 128), F32),
            pltpu.VMEM((BLOCKS, 128), F32),
            pltpu.SMEM((BLOCKS, 128), F32),
            pltpu.VMEM((BLOCKS, 8, WIDTH + 128), BF16),
            pltpu.VMEM((256, 768), BF16),
            pltpu.VMEM((6, ROWS, 128), F32),
            pltpu.SemaphoreType.DMA,
            pltpu.SemaphoreType.DMA,
            pltpu.SemaphoreType.DMA,
            pltpu.SemaphoreType.DMA,
            pltpu.SemaphoreType.DMA,
            pltpu.SemaphoreType.DMA,
            pltpu.SemaphoreType.DMA((CHUNKS,)),
            pltpu.SemaphoreType.DMA((CHUNKS,)),
            pltpu.SemaphoreType.DMA((CHUNKS,)),
            pltpu.SemaphoreType.DMA((CHUNKS,)),
        ],
        compiler_params=pltpu.CompilerParams(
            collective_id=0, has_side_effects=True, vmem_limit_bytes=32 << 20
        ),
        name="coadd_match",
    )(
        in_hbm(block_dest), in_hbm(band_offset), in_hbm(col_shift), in_hbm(block_weight),
        in_hbm(basis_width), in_hbm(kernel_fit.transpose(1, 0, 2)), fit_owner,
        in_hbm(exposure.reshape(BLOCKS, 8, COLS)),
    )
    return matched, cover.reshape(BLOCKS)


def solution(mesh):
    row_spec = P(("det", "patch"))
    in_specs = (
        P(("det", "patch"), None), row_spec, row_spec, row_spec, row_spec,
        P(), P(("det", "patch"), None, None), P(),
    )
    out_specs = (P(("det", "patch"), None), row_spec)
    return jax.shard_map(shards, mesh=mesh, in_specs=in_specs, out_specs=out_specs, check_vma=False)
```

time: 96 us -> 58.6 us (0.61)
  the two profiles are of different devices: /device:TPU:0 before, /device:TPU:1 now
where the time goes in v2:
time: 58.6 us; the launch traced here: 58.5 us
  Pallas kernels  55.3 us (94%)
  local copies, waits for them, and re-layouts  1.83 us (3%)
  between operations  1.29 us (2%)
    pallas_call x1, Pallas kernels, shards(): pl.pallas_call(kernel, out_shape=(jax.ShapeDtypeStruct((ROWS, COLS), BF16...  55.3 us
    unnamed x2, local copies, waits for them, and re-layouts  1.83 us

profile of v2, /device:TPU:1, one launch (start us, length us, event | category | flops | bytes accessed | tf_op | source)
XLA Modules:
  0.0 58.5 jit_solution(12699326879925115953)
XLA Ops:
  1.3 55.3 %coadd_match.1 = (bf16[256,4096]{1,0:T(8,128)(2,1)S(1)}, f32[1,32]{1,0:T(1,128)S(1)}) custom-call(s32[32]{0:T(128)} %dest_hbm.1, s32[32]{0:T(128)} %offset_hbm.1, f32[32]{0:T(128)} %shift_hbm.1, f32[32]{0:T(128)} %weight_hbm.1, f32[3]{0:T(128)} %width_hbm.1, f32[3,1,6]{2,1,0:T(1,128)} %bitcast.5, s32[1]{0:T(128)S(6)} %copy.12.owner_ref, ...), custom_call_target="tpu_custom_call" | custom-call | tf_op jit(solution)/shard_map/coadd_match/pallas_call | solution.py:416
  56.6 1.3 %copy.13 = bf16[256,4096]{1,0:T(8,128)(2,1)} copy(bf16[256,4096]{1,0:T(8,128)(2,1)S(1)} %get-tuple-element.8) | data formatting | bytes 4194304
  58.0 0.5 copy.14

commit v3 on v2

--- a/solution.py
+++ b/solution.py
@@ -14,12 +14,14 @@
 NPOLY = 6
 COLS = 4096
 CHUNKS = 8
-WINDOW = 3
+WINDOW = 5
 UNROLL = 16
 LEAD = 9
-LAG = 2
+FIRST = 1024
+LAG = 4
 WIDTH = COLS // CHUNKS
 TILES = WIDTH // 128
+PER = WIDTH // 256
 BLOCKS = 32
 ROWS = 256
 PEERS = 16
@@ -53,9 +55,9 @@
     out_ref, cover_ref,
     dest_ref, offset_ref, shift_ref, weight_ref, width_ref, fit_ref, small_sem,
     padded, weighted, packed, arrived, meta_out, meta_in, fit_out, fit_in, edges,
-    pack_mat, row_mat, edge_mat, band_mat, rowconv, y_cols, edge_scale, coef_table, coef_ref,
+    pack_mat, row_mat, rim_mat, edge_mat, band_mat, rowconv, y_cols, edge_scale, coef_table,
     moved, shift_mat, coef_wide,
-    load_sem, coef_sem, fit_send, fit_recv, meta_send, meta_recv, bulk_send, bulk_recv, edge_send, edge_recv,
+    load_sem, rest_sem, fit_send, fit_recv, meta_send, meta_recv, bulk_send, bulk_recv, edge_send, edge_recv,
 ):
     det = lax.axis_index("det")
     pat = lax.axis_index("patch")
@@ -65,8 +67,6 @@
     after_id = (after // PEERS, lax.rem(after, PEERS))
     before_id = (before // PEERS, lax.rem(before, PEERS))
 
-    load = pltpu.make_async_copy(exposure_ref, padded.at[:, :, 128 : 128 + COLS], load_sem)
-    load.start()
     smalls = [
         pltpu.make_async_copy(source, target, small_sem.at[i])
         for i, (source, target) in enumerate(
@@ -79,6 +79,14 @@
     ]
     for copy in smalls:
         copy.start()
+    load = pltpu.make_async_copy(
+        exposure_ref.at[:, :, 0:FIRST], padded.at[:, :, 128 : 128 + FIRST], load_sem
+    )
+    load.start()
+    rest = pltpu.make_async_copy(
+        exposure_ref.at[:, :, FIRST:], padded.at[:, :, 128 + FIRST : 128 + COLS], rest_sem
+    )
+    rest.start()
 
     barrier = pltpu.get_barrier_semaphore()
 
@@ -111,18 +119,6 @@
         heavy = jnp.where(deep == b, weight_ref[b], heavy)
     position = (iota((BLOCKS, 128), 1) - 2).astype(F32) - shift
     coef_table[...] = sinc(position) * sinc(position / 3.0) * heavy
-    coef_copy = pltpu.make_async_copy(coef_table, coef_ref, coef_sem)
-    coef_copy.start()
-
-    mine = jnp.where(owner_ref[0] == dev, 1.0, 0.0)
-    lane_1 = iota((8, 128), 1)
-    fit_row = jnp.zeros((8, 128), F32)
-    for k in range(BASES):
-        for n in range(NPOLY):
-            fit_row = jnp.where(lane_1 == FIT_LANE + k * NPOLY + n, fit_ref[k, 0, n], fit_row)
-    fit_row = jnp.where(mine > 0.5, fit_row, 0.0)
-    fit_out[...] = fit_row
-    fit_in[det] = fit_row
 
     lane = iota((1, ROWS), 1)
     owner_block = lane // 8
@@ -143,11 +139,6 @@
     target = rank * 128 + peer * 8 + phase
     select = jnp.where(iota((PACKED, ROWS), 0) == target, 1.0, 0.0)
     pack_mat[...] = select.astype(BF16)
-    row_value = (slot * 8 + phase + 1).astype(F32)
-    row_col = jnp.sum(select * row_value, axis=1, keepdims=True)
-    weight_col = jnp.sum(select * weight, axis=1, keepdims=True)
-
-
     def resample(chunk):
         start = pl.multiple_of(chunk * WIDTH, 128)
 
@@ -203,13 +194,62 @@
     spot = iota((256, 768), 1)
     reads = lax.rem(spot, 128) + spot // 128 + (LEAD - 2)
     shift_mat[...] = jnp.where(iota((256, 768), 0) == reads, 1.0, 0.0).astype(BF16)
-    coef_copy.wait()
     for b in range(BLOCKS):
+        row = jnp.broadcast_to(coef_table[b : b + 1, :], (8, 128))
         for i in range(6):
-            coef_wide[i, b * 8 : (b + 1) * 8, :] = jnp.full((8, 128), coef_ref[b, i], F32)
+            coef_wide[i, b * 8 : (b + 1) * 8, :] = jnp.broadcast_to(row[:, i : i + 1], (8, 128))
     load.wait()
 
     resample(0)
+
+    mine = jnp.where(owner_ref[0] == dev, 1.0, 0.0)
+    lane_1 = iota((8, 128), 1)
+    fit_row = jnp.zeros((8, 128), F32)
+    for k in range(BASES):
+        for n in range(NPOLY):
+            fit_row = jnp.where(lane_1 == FIT_LANE + k * NPOLY + n, fit_ref[k, 0, n], fit_row)
+    fit_row = jnp.where(mine > 0.5, fit_row, 0.0)
+    fit_out[...] = fit_row
+    fit_in[det] = fit_row
+
+    pl.semaphore_wait(barrier, PEERS - 1 + GROUPS - 1 + 2)
+
+    @pl.loop(1, GROUPS)
+    def _(step):
+        pltpu.make_async_remote_copy(
+            fit_out, fit_in.at[det], fit_send, fit_recv,
+            device_id=(lax.rem(det + step, GROUPS), pat), device_id_type=MESH,
+        ).start()
+
+    send(0)
+    rest.wait()
+    row_value = (slot * 8 + phase + 1).astype(F32)
+    row_col = jnp.sum(select * row_value, axis=1, keepdims=True)
+    weight_col = jnp.sum(select * weight, axis=1, keepdims=True)
+    whole = fit_in.at[0 : GROUPS - 1]
+    pltpu.make_async_copy(whole, whole, fit_recv).wait()
+    chosen = jnp.sum(fit_in[...], axis=0)
+    lanes_m = iota((128, 128), 1)
+    meta = jnp.broadcast_to(chosen[0:1, :], (128, 128))
+    for r in range(RANKS):
+        part = slice(r * 128, (r + 1) * 128)
+        meta = jnp.where(lanes_m == r, row_col[part], meta)
+        meta = jnp.where(lanes_m == RANKS + r, weight_col[part], meta)
+    meta_out[...] = meta.reshape(PEERS, 8, 128)
+    pltpu.make_async_copy(meta_out.at[pat], meta_in.at[pat], meta_recv).start()
+
+    @pl.loop(1, PEERS)
+    def _(step):
+        other = lax.rem(pat + step, PEERS)
+        pltpu.make_async_remote_copy(
+            meta_out.at[other], meta_in.at[pat], meta_send, meta_recv,
+            device_id=(det, other), device_id_type=MESH,
+        ).start()
+
+    @pl.loop(1, WINDOW)
+    def _(chunk):
+        resample(chunk)
+        send(chunk)
 
     span = iota((8, 128), 1).astype(F32) - HALF
     norms = []
@@ -224,41 +264,6 @@
     for k in range(BASES):
         rowconv[k, :, 0:128] = jnp.zeros((ROWS, 128), BF16)
         rowconv[k, :, 128 + COLS :] = jnp.zeros((ROWS, 128), BF16)
-
-    pl.semaphore_wait(barrier, PEERS - 1 + GROUPS - 1 + 2)
-
-    @pl.loop(1, GROUPS)
-    def _(step):
-        pltpu.make_async_remote_copy(
-            fit_out, fit_in.at[det], fit_send, fit_recv,
-            device_id=(lax.rem(det + step, GROUPS), pat), device_id_type=MESH,
-        ).start()
-
-    send(0)
-    whole = fit_in.at[0 : GROUPS - 1]
-    pltpu.make_async_copy(whole, whole, fit_recv).wait()
-    chosen = jnp.sum(fit_in[...], axis=0)
-    lanes_m = iota((128, 128), 1)
-    meta = jnp.broadcast_to(chosen[0:1, :], (128, 128))
-    for r in range(RANKS):
-        part = slice(r * 128, (r + 1) * 128)
-        meta = jnp.where(lanes_m == r, row_col[part], meta)
-        meta = jnp.where(lanes_m == RANKS + r, weight_col[part], meta)
-    meta_out[...] = meta.reshape(PEERS, 8, 128)
-    pltpu.make_async_copy(meta_out.at[pat], meta_in.at[pat], meta_recv).start()
-
-    @pl.loop(1, PEERS)
-    def _(step):
-        other = lax.rem(pat + step, PEERS)
-        pltpu.make_async_remote_copy(
-            meta_out.at[other], meta_in.at[pat], meta_send, meta_recv,
-            device_id=(det, other), device_id_type=MESH,
-        ).start()
-
-    @pl.loop(1, WINDOW)
-    def _(chunk):
-        resample(chunk)
-        send(chunk)
 
     pltpu.make_async_copy(meta_in, meta_in, meta_recv).wait()
     meta_got = meta_in[...].reshape(128, 128)
@@ -286,7 +291,10 @@
         spread = lax.dot_general(inner, lands, contract, preferred_element_type=F32)
         row_mat[k * ROWS : (k + 1) * ROWS, 0:PACKED] = spread.astype(BF16)
         outer = gaussian(rim_reach, width_ref[k], norms[k]) * rim_live
-        row_mat[k * ROWS : (k + 1) * ROWS, PACKED:] = outer.astype(BF16)
+        for n, at in enumerate((0, ROWS - EDGE)):
+            place = slice((2 * k + n) * EDGE, (2 * k + n + 1) * EDGE)
+            rim_mat[place, 0:PACKED] = spread[at : at + EDGE].astype(BF16)
+            rim_mat[place, PACKED:] = outer[at : at + EDGE].astype(BF16)
     edge_i = iota((2 * EDGE, ROWS), 0)
     edge_row = jnp.where(edge_i < EDGE, edge_i, edge_i + ROWS - 2 * EDGE)
     picks = jnp.where(edge_row == iota((2 * EDGE, ROWS), 1), 1.0, 0.0)
@@ -325,18 +333,31 @@
         for copy in edge_copies(chunk):
             copy.start()
 
-    def row_stage(chunk):
+    def rims_in(chunk):
         rims = arrived.at[chunk, RANKS, 0:4]
         pltpu.make_async_copy(rims, rims, edge_recv.at[chunk]).wait()
+
+    def columns(chunk):
+        return pl.ds(pl.multiple_of(128 + chunk * WIDTH, 128), WIDTH)
+
+    def row_stage(chunk):
+        got = arrived[chunk, 0:RANKS].reshape(PACKED, WIDTH)
+        for k in range(BASES):
+            value = jnp.dot(
+                row_mat[k * ROWS : (k + 1) * ROWS, 0:PACKED], got, preferred_element_type=F32
+            )
+            rowconv[k, :, columns(chunk)] = value.astype(BF16)
+
+    def row_rims(chunk):
         got = arrived[chunk, 0:RANKS].reshape(PACKED, WIDTH)
         rim_rows = arrived[chunk, RANKS, 0:4].reshape(2 * EDGE, WIDTH)
         full = jnp.concatenate([got, rim_rows], axis=0)
-        at = pl.ds(pl.multiple_of(128 + chunk * WIDTH, 128), WIDTH)
+        value = jnp.dot(rim_mat[...], full, preferred_element_type=F32).astype(BF16)
         for k in range(BASES):
-            value = jnp.dot(
-                row_mat[k * ROWS : (k + 1) * ROWS, :], full, preferred_element_type=F32
-            )
-            rowconv[k, :, at] = value.astype(BF16)
+            top = value[2 * k * EDGE : (2 * k + 1) * EDGE]
+            low = value[(2 * k + 1) * EDGE : (2 * k + 2) * EDGE]
+            rowconv[k, 0:EDGE, columns(chunk)] = top
+            rowconv[k, ROWS - EDGE : ROWS, columns(chunk)] = low
 
     terms = [
         [
@@ -349,22 +370,35 @@
         for k in range(BASES)
     ]
 
-    def col_tile(tile):
-        at = pl.multiple_of(tile * 256, 128)
+    def matched_rows(tile, y, take):
         x = 2.0 * (tile * 256 + iota((1, 256), 1)).astype(F32) / (COLS - 1) - 1.0
-        y = y_cols[:, 0:1]
         result = None
         for k in range(BASES):
-            value = jnp.dot(
-                rowconv[k, :, pl.ds(at, 512)], band_mat[k], preferred_element_type=F32
-            )
+            value = jnp.dot(take(k), band_mat[k], preferred_element_type=F32)
             a = terms[k]
             level = a[0] + a[1] * x + a[3] * x * x
             slope = a[2] + a[4] * x
             field = level + y * slope + (a[5] * y) * y
             part = field * value
             result = part if result is None else result + part
-        out_ref[:, pl.ds(at, 256)] = result.astype(BF16)
+        return result.astype(BF16)
+
+    def col_tile(tile):
+        at = pl.multiple_of(tile * 256, 128)
+        out_ref[:, pl.ds(at, 256)] = matched_rows(
+            tile, y_cols[:, 0:1], lambda k: rowconv[k, :, pl.ds(at, 512)]
+        )
+
+    def col_rims(tile):
+        at = pl.multiple_of(tile * 256, 128)
+        sides = (slice(0, EDGE), slice(ROWS - EDGE, ROWS))
+        y = jnp.concatenate([y_cols[side, 0:1] for side in sides], axis=0)
+        result = matched_rows(
+            tile, y,
+            lambda k: jnp.concatenate([rowconv[k, side, pl.ds(at, 512)] for side in sides], axis=0),
+        )
+        for n, side in enumerate(sides):
+            out_ref[side, pl.ds(at, 256)] = result[n * EDGE : (n + 1) * EDGE]
 
     @pl.loop(0, CHUNKS)
     def _(chunk):
@@ -380,20 +414,33 @@
         def _():
             send(chunk + WINDOW)
 
+        row_stage(chunk)
+
+        @pl.when(chunk > 0)
+        def _():
+            col_tile(PER * chunk - 1)
+
+        for back in range(PER - 1):
+            col_tile(PER * chunk + back)
+
         @pl.when(chunk >= LAG)
         def _():
-            row_stage(chunk - LAG)
-            col_tile(2 * (chunk - LAG))
+            rims_in(chunk - LAG)
+            row_rims(chunk - LAG)
+            for back in range(PER - 1):
+                col_rims(PER * (chunk - LAG) + back)
 
         @pl.when(chunk > LAG)
         def _():
-            col_tile(2 * (chunk - LAG) - 1)
-
+            col_rims(PER * (chunk - LAG) - 1)
+
+    col_tile(PER * CHUNKS - 1)
     for last in range(CHUNKS - LAG, CHUNKS):
-        row_stage(last)
-        col_tile(2 * last - 1)
-        col_tile(2 * last)
-    col_tile(2 * CHUNKS - 1)
+        rims_in(last)
+        row_rims(last)
+        for back in range(-1, PER - 1):
+            col_rims(PER * last + back)
+    col_rims(PER * CHUNKS - 1)
 
     pltpu.make_async_copy(whole, whole, fit_send).wait()
     sent = meta_out.at[0 : PEERS - 1]
@@ -439,14 +486,14 @@
             pltpu.VMEM((GROUPS, 8, 128), F32),
             pltpu.VMEM((CHUNKS, 4, 8, WIDTH), BF16),
             pltpu.VMEM((PACKED, ROWS), BF16),
-            pltpu.VMEM((BASES * ROWS, PACKED + 2 * EDGE), BF16),
+            pltpu.VMEM((BASES * ROWS, PACKED), BF16),
+            pltpu.VMEM((BASES * 2 * EDGE, PACKED + 2 * EDGE), BF16),
             pltpu.VMEM((2 * EDGE, PACKED), BF16),
             pltpu.VMEM((BASES, 512, 256), BF16),
             pltpu.VMEM((BASES, ROWS, COLS + 256), BF16),
             pltpu.VMEM((ROWS, 128), F32),
             pltpu.VMEM((2 * EDGE, 128), F32),
             pltpu.VMEM((BLOCKS, 128), F32),
-            pltpu.SMEM((BLOCKS, 128), F32),
             pltpu.VMEM((BLOCKS, 8, WIDTH + 128), BF16),
             pltpu.VMEM((256, 768), BF16),
             pltpu.VMEM((6, ROWS, 128), F32),

time: 58.6 us -> 57.2 us (0.976)
  Pallas kernels: 55.3 us -> 54 us
    pallas_call x1, Pallas kernels: 55.3 us -> 54 us  [shards(): pl.pallas_call(kernel, out_shape=(jax.ShapeDtypeStruct((ROWS, COLS), BF16...]
where the time goes in v3:
time: 57.2 us; the launch traced here: 57.1 us
  Pallas kernels  54 us (94%)
  local copies, waits for them, and re-layouts  1.83 us (3%)
  between operations  1.29 us (2%)
    pallas_call x1, Pallas kernels, shards(): pl.pallas_call(kernel, out_shape=(jax.ShapeDtypeStruct((ROWS, COLS), BF16...  54 us
    unnamed x2, local copies, waits for them, and re-layouts  1.83 us

profile of v3, /device:TPU:1, one launch (start us, length us, event | category | flops | bytes accessed | tf_op | source)
XLA Modules:
  0.0 57.1 jit_solution(9314144230419567787)
XLA Ops:
  1.3 54.0 %coadd_match.1 = (bf16[256,4096]{1,0:T(8,128)(2,1)S(1)}, f32[1,32]{1,0:T(1,128)S(1)}) custom-call(s32[32]{0:T(128)} %dest_hbm.1, s32[32]{0:T(128)} %offset_hbm.1, f32[32]{0:T(128)} %shift_hbm.1, f32[32]{0:T(128)} %weight_hbm.1, f32[3]{0:T(128)} %width_hbm.1, f32[3,1,6]{2,1,0:T(1,128)} %bitcast.5, s32[1]{0:T(128)S(6)} %copy.12.owner_ref, ...), custom_call_target="tpu_custom_call" | custom-call | tf_op jit(solution)/shard_map/coadd_match/pallas_call | solution.py:463
  55.2 1.3 %copy.13 = bf16[256,4096]{1,0:T(8,128)(2,1)} copy(bf16[256,4096]{1,0:T(8,128)(2,1)S(1)} %get-tuple-element.8) | data formatting | bytes 4194304
  56.6 0.5 copy.14

commit v4 on v3

--- a/solution.py
+++ b/solution.py
@@ -402,13 +402,13 @@
 
     @pl.loop(0, CHUNKS)
     def _(chunk):
+        wait_bulk(chunk)
+
+        make_edges(chunk)
+
         @pl.when(chunk + WINDOW < CHUNKS)
         def _():
             resample(chunk + WINDOW)
-
-        wait_bulk(chunk)
-
-        make_edges(chunk)
 
         @pl.when(chunk + WINDOW < CHUNKS)
         def _():

time: 57.2 us -> 57.2 us (level)
  no operation moved by 1% of the time
where the time goes in v4:
time: 57.2 us; the launch traced here: 57.1 us
  Pallas kernels  54 us (94%)
  local copies, waits for them, and re-layouts  1.83 us (3%)
  between operations  1.29 us (2%)
    pallas_call x1, Pallas kernels, shards(): pl.pallas_call(kernel, out_shape=(jax.ShapeDtypeStruct((ROWS, COLS), BF16...  54 us
    unnamed x2, local copies, waits for them, and re-layouts  1.83 us

profile of v4, /device:TPU:1, one launch (start us, length us, event | category | flops | bytes accessed | tf_op | source)
XLA Modules:
  0.0 57.1 jit_solution(14979401512553508742)
XLA Ops:
  1.3 54.0 %coadd_match.1 = (bf16[256,4096]{1,0:T(8,128)(2,1)S(1)}, f32[1,32]{1,0:T(1,128)S(1)}) custom-call(s32[32]{0:T(128)} %dest_hbm.1, s32[32]{0:T(128)} %offset_hbm.1, f32[32]{0:T(128)} %shift_hbm.1, f32[32]{0:T(128)} %weight_hbm.1, f32[3]{0:T(128)} %width_hbm.1, f32[3,1,6]{2,1,0:T(1,128)} %bitcast.5, s32[1]{0:T(128)S(6)} %copy.12.owner_ref, ...), custom_call_target="tpu_custom_call" | custom-call | tf_op jit(solution)/shard_map/coadd_match/pallas_call | solution.py:463
  55.2 1.3 %copy.13 = bf16[256,4096]{1,0:T(8,128)(2,1)} copy(bf16[256,4096]{1,0:T(8,128)(2,1)S(1)} %get-tuple-element.8) | data formatting | bytes 4194304
  56.6 0.5 copy.14
